TPU v7x, 32 devices: a whole 2x2x4 slice. The times are simulated.
32 devices in a mesh: row: 2 (over x), col: 4 (over y, core), rhs: 4 (over z).
Axes of the slice: x: 2, y: 2, z: 4, core: 2. Of those that a mesh axis runs over, the one named last changes fastest.
Arguments:
- right_side: float32 [2, 64, 8192], P('row', 'rhs', 'col'), may hold values from -6 to 6
- guess: float32 [2, 64, 8192], P('row', 'rhs', 'col'), may hold values from -6 to 6
- inverse: bfloat16 [2, 8192, 8192], P('row', 'rhs', 'col'), may hold values from -0.0625 to 0.0625
- left_factor: bfloat16 [2, 2, 64, 8192], P('row', None, None, 'col'), may hold values from -0.5 to 0.5
- right_factor: bfloat16 [2, 2, 64, 8192], P('row', None, None, 'col'), may hold values from -0.0625 to 0.0625
- ranks: int32 [2, 2], replicated, may hold values from 16 to 64
Outputs:
- solution: float32 [2, 64, 8192], P('row', 'rhs', 'col')
Inputs may be any that keep to these rules, and one draw needn't show every extreme that they name: ranks[i, j] is the rank of the block in block row i and block column j; diagonal entries are not read.
All inputs are finite; a program needn't handle non-finite values.
Results may differ from a plain program's by a relative error of at most 0.008.
Values may be sent and summed in bfloat16 or wider, within the bound.
A program may use at most 128 MiB of HBM per device.

v0:
```python
import jax
import jax.numpy as jnp
from jax import lax
from jax.sharding import PartitionSpec as P


def body(right_side, guess, inverse, left_factor, right_factor, ranks):
    blocks = lax.axis_size("row")
    mine = lax.axis_index("row")
    left = left_factor[0]
    right = right_factor[0]
    width = left.shape[1]
    keep = (lax.broadcasted_iota(jnp.int32, (blocks, blocks, width), 2) < ranks[:, :, None]).astype(
        jnp.float32
    )
    keep_mine = lax.dynamic_index_in_dim(keep, mine, 1, keepdims=False)
    partial_value = jnp.einsum(
        "rm,ikm->irk", guess[0].astype(jnp.bfloat16), right, preferred_element_type=jnp.float32
    )
    partial_value = partial_value * keep_mine[:, None, :]
    old_sum = lax.psum(partial_value, "col").astype(jnp.bfloat16)
    old_mine = lax.all_to_all(old_sum, "row", split_axis=0, concat_axis=0, tiled=True)
    later = lax.broadcasted_iota(jnp.int32, (blocks, 1, 1), 0) > mine
    old_kept = jnp.where(later, old_mine, jnp.zeros_like(old_mine))
    upper = jnp.einsum("jrk,jkm->rm", old_kept, left, preferred_element_type=jnp.float32)
    base = right_side[0] - upper
    lower = jnp.zeros_like(base)
    solution = jnp.zeros_like(base)
    for step in range(blocks):
        residue = (base - lower).astype(jnp.bfloat16)
        residue_full = lax.all_gather(residue, "col", axis=1, tiled=True)
        pieces = lax.all_to_all(residue_full, "rhs", split_axis=1, concat_axis=0, tiled=True)
        product = jnp.dot(pieces, inverse[0], preferred_element_type=jnp.float32)
        current = lax.psum_scatter(product, "rhs", scatter_dimension=0, tiled=True)
        solution = jnp.where(mine == step, current, solution)
        if step + 1 < blocks:
            coef = jnp.einsum(
                "rm,ikm->irk",
                current.astype(jnp.bfloat16),
                right,
                preferred_element_type=jnp.float32,
            )
            coef = coef * keep[:, step][:, None, :]
            coef = jnp.where(mine == step, coef, jnp.zeros_like(coef))
            shared = lax.psum(coef, ("row", "col")).astype(jnp.bfloat16)
            own_coef = lax.dynamic_index_in_dim(shared, mine, 0, keepdims=False)
            term = jnp.dot(own_coef, left[step], preferred_element_type=jnp.float32)
            lower = lower + jnp.where(mine > step, term, jnp.zeros_like(term))
    return solution[None]


def solution(mesh):
    in_specs = (
        P("row", "rhs", "col"),
        P("row", "rhs", "col"),
        P("row", "rhs", "col"),
        P("row", None, None, "col"),
        P("row", None, None, "col"),
        P(),
    )
    out_specs = P("row", "rhs", "col")
    return jax.shard_map(body, mesh=mesh, in_specs=in_specs, out_specs=out_specs, check_vma=False)
```

profile of v0, /device:TPU:2, one launch (start us, length us, event | category | flops | bytes accessed | tf_op | source)
XLA Modules:
  0.0 149.9 jit_solution(729392228866643291)
XLA Ops:
  6.5 0.0 copy-start
  6.5 0.8 copy.8
  7.4 0.1 compare_convert_fusion
  7.4 0.2 copy-done
  7.6 1.2 fusion.9
  8.8 11.3 %psum.14 = bf16[2,16,64]{2,1,0:T(8,128)(2,1)S(1)} all-reduce(f32[2,16,64]{2,1,0:T(8,128)S(1)} %fusion.9), channel_id=1, replica_groups=mesh['row'=2,'col'=4,'rhs'=4] {'col'}, use_global_device_ids=true, to_apply=%region_0.1 | all-reduce | flops 2048 | bytes 12288 | tf_op jit(solution)/shard_map/psum | solution.py:21
  20.1 0.7 reshape.18
  20.7 3.7 %all-to-all-start = ((bf16[2,2,512]{2,1,0:T(2,128)(2,1)}), bf16[2,2,512]{2,1,0:T(2,128)(2,1)S(1)}, u32[]{:S(2)}, u32[]{:S(2)}) async-start(bf16[2,2,512]{2,1,0:T(2,128)(2,1)} %reshape.18), calls=%async_computation | async-start | bytes 8192 | tf_op jit(solution)/shard_map/all_to_all | solution.py:22
  24.5 0.0 reduce-scatter.3.cloned.1.call-start
  24.5 1.8 %all-to-all-done = bf16[2,2,512]{2,1,0:T(2,128)(2,1)S(1)} async-done(((bf16[2,2,512]{2,1,0:T(2,128)(2,1)}), bf16[2,2,512]{2,1,0:T(2,128)(2,1)S(1)}, u32[]{:S(2)}, u32[]{:S(2)}) %all-to-all-start) | async-done | bytes 4128 | tf_op jit(solution)/shard_map/all_to_all | solution.py:22
  26.3 0.1 reshape.19
  26.4 1.4 fusion.26
  27.7 5.8 %all_gather.6 = bf16[16,8192]{1,0:T(8,128)(2,1)S(1)} all-gather(bf16[16,2048]{1,0:T(8,128)(2,1)S(1)} %get-tuple-element.7), channel_id=1, replica_groups=mesh['row'=2,'col'=4,'rhs'=4] {'col'}, dimensions={1}, use_global_device_ids=true | all-gather | bytes 327680 | tf_op jit(solution)/shard_map/all_gather | solution.py:31
  33.5 14.1 %all_to_all.43 = bf16[16,4,2048]{2,0,1:T(8,128)(2,1)S(1)} all-to-all(bf16[16,4,2048]{2,0,1:T(8,128)(2,1)S(1)} %bitcast.64), channel_id=1, replica_groups=mesh['row'=2,'col'=4,'rhs'=4] {'rhs'}, dimensions={1} | all-to-all | bytes 524288 | tf_op jit(solution)/shard_map/all_to_all | solution.py:32
  47.6 0.0 copy-start.1
  47.6 5.8 %fusion.2 = f32[64,2048]{1,0:T(8,128)} fusion(bf16[64,2048]{1,0:T(8,128)(2,1)S(1)} %bitcast.60, bf16[1,2048,2048]{2,1,0:T(8,128)(2,1)} %param.8), kind=kOutput, calls=%fused_computation.2 | convolution fusion | flops 536870912 | bytes 9175040 | tf_op jit(solution)/shard_map/dot_general | solution.py:33
  53.4 0.0 reduce-scatter.3.cloned.1.call-update
  53.4 0.0 reduce-scatter.5.cloned.1.call-start
  53.5 20.5 %reduce-scatter.3.cloned.1.call-done = f32[16,2048]{1,0:T(8,128)} async-done(((f32[64,2048]{1,0:T(8,128)}), f32[16,2048]{1,0:T(8,128)}) %reduce-scatter.3.cloned.1.call-update) | async-done | bytes 131088 | tf_op jit(solution)/shard_map/reduce_scatter | solution.py:34
  74.0 1.2 fusion.8
  75.2 22.4 %psum.15 = bf16[2,16,64]{2,1,0:T(8,128)(2,1)S(1)} all-reduce(f32[2,16,64]{2,1,0:T(8,128)S(1)} %fusion.8), channel_id=1, replica_groups=mesh['row'=2,'col'=4,'rhs'=4] {'row','col'}, use_global_device_ids=true, to_apply=%region_2.3 | all-reduce | flops 2048 | bytes 12288 | tf_op jit(solution)/shard_map/psum | solution.py:45
  97.6 0.0 copy-done.1
  97.6 0.2 fusion.6
  97.7 5.8 %all_gather.7 = bf16[16,8192]{1,0:T(8,128)(2,1)S(1)} all-gather(bf16[16,2048]{1,0:T(8,128)(2,1)S(1)} %fusion.6), channel_id=1, replica_groups=mesh['row'=2,'col'=4,'rhs'=4] {'col'}, dimensions={1}, use_global_device_ids=true | all-gather | bytes 327680 | tf_op jit(solution)/shard_map/all_gather | solution.py:31
  103.5 12.0 %all_to_all.44 = bf16[16,4,2048]{2,0,1:T(8,128)(2,1)S(1)} all-to-all(bf16[16,4,2048]{2,0,1:T(8,128)(2,1)S(1)} %bitcast.65), channel_id=1, replica_groups=mesh['row'=2,'col'=4,'rhs'=4] {'rhs'}, dimensions={1} | all-to-all | bytes 524288 | tf_op jit(solution)/shard_map/all_to_all | solution.py:32
  115.6 0.0 copy-start.2
  115.6 5.8 %fusion = f32[64,2048]{1,0:T(8,128)} fusion(bf16[64,2048]{1,0:T(8,128)(2,1)S(1)} %bitcast.61, bf16[1,2048,2048]{2,1,0:T(8,128)(2,1)} %param.8), kind=kOutput, calls=%fused_computation | convolution fusion | flops 536870912 | bytes 9175040 | tf_op jit(solution)/shard_map/dot_general | solution.py:33
  121.4 0.0 reduce-scatter.5.cloned.1.call-update
  121.4 20.1 %reduce-scatter.5.cloned.1.call-done = f32[16,2048]{1,0:T(8,128)} async-done(((f32[64,2048]{1,0:T(8,128)}), f32[16,2048]{1,0:T(8,128)}) %reduce-scatter.5.cloned.1.call-update) | async-done | bytes 131088 | tf_op jit(solution)/shard_map/reduce_scatter | solution.py:34
  141.5 0.0 copy-done.2
  141.5 1.6 %select_bitcast_fusion = f32[1,16,2048]{2,1,0:T(8,128)} fusion(f32[16,2048]{1,0:T(8,128)} %reduce-scatter.5.cloned.1.call-done, f32[16,2048]{1,0:T(8,128)S(1)} %copy-done.2, pred[]{:T(512)S(6)} %eq.8, pred[]{:T(512)S(6)} %eq.7), kind=kLoop, calls=%fused_computation.21 | loop fusion | flops 65536 | bytes 393218 | tf_op jit(solution)/shard_map/broadcast_in_dim | solution.py:49
  (4 shorter events, 0.0 us)
Async XLA Ops:
  6.5 1.1 copy-start
  20.7 5.5 %all-to-all-start = ((bf16[2,2,512]{2,1,0:T(2,128)(2,1)}), bf16[2,2,512]{2,1,0:T(2,128)(2,1)S(1)}, u32[]{:S(2)}, u32[]{:S(2)}) async-start(bf16[2,2,512]{2,1,0:T(2,128)(2,1)} %reshape.18), calls=%async_computation | async-start | bytes 8192 | tf_op jit(solution)/shard_map/all_to_all | solution.py:22
  24.5 49.5 %reduce-scatter.3.cloned.1.call-start = ((), (), s32[]{:S(2)}) async-start(), calls=%async_computation.5 | async-start | bytes 655360 | tf_op jit(solution)/shard_map/reduce_scatter | solution.py:34
  47.6 50.0 %copy-start.1 = (bf16[1,2,64,2048]{3,2,1,0:T(8,128)(2,1)S(1)}, bf16[1,2,64,2048]{3,2,1,0:T(8,128)(2,1)}, u32[]{:S(2)}) copy-start(bf16[1,2,64,2048]{3,2,1,0:T(8,128)(2,1)} %param.9) | copy-start | bytes 1572868
  53.4 88.1 %reduce-scatter.5.cloned.1.call-start = ((), (), s32[]{:S(2)}) async-start(), calls=%async_computation.6 | async-start | bytes 655360 | tf_op jit(solution)/shard_map/reduce_scatter | solution.py:34
  115.6 25.9 %copy-start.2 = (f32[16,2048]{1,0:T(8,128)S(1)}, f32[16,2048]{1,0:T(8,128)}, u32[]{:S(2)}) copy-start(f32[16,2048]{1,0:T(8,128)} %reduce-scatter.3.cloned.1.call-done) | copy-start | bytes 393220
Sparse Core Ops, SparseCore 0:
  53.5 20.4 reduce-scatter.2
  121.5 19.9 reduce-scatter.4
where the time goes:
time: 151 us; the launch traced here: 150 us
  blocking collectives  71.3 us (47%)
  waiting for transfers between devices  42.4 us (28%)
  matrix products  15.5 us (10%)
  between operations  13.4 us (9%)
  starting transfers between devices  3.79 us (3%)
  local copies, waits for them, and re-layouts  1.79 us (1%)
  other arithmetic  1.65 us (1%)
    reduce_scatter x2, waiting for transfers between devices, body(): current = lax.psum_scatter(product, 'rhs', scatter_dimension=0, tiled=True)  40.6 us
    all_to_all x2, blocking collectives, body(): lax.all_to_all(residue_full, 'rhs', split_axis=1, concat_axis=0, tiled=True)  26.1 us
    psum x1, blocking collectives, body(): shared = lax.psum(coef, ('row', 'col')).astype(jnp.bfloat16)  22.4 us
    dot_general x2, matrix products, body(): product = jnp.dot(pieces, inverse[0], preferred_element_type=jnp.float32)  11.6 us
    all_gather x2, blocking collectives, body(): residue_full = lax.all_gather(residue, 'col', axis=1, tiled=True)  11.6 us
    psum x1, blocking collectives, body(): old_sum = lax.psum(partial_value, 'col').astype(jnp.bfloat16)  11.3 us
    all_to_all x1, starting transfers between devices, body(): lax.all_to_all(old_sum, 'row', split_axis=0, concat_axis=0, tiled=True)  3.74 us
  transfers between devices with their start and end apart: 3, of which 3 were waited for; matrix products, arithmetic and copies ran while one was open for 0% of the time, Pallas kernels for 0%

commit v1 on v0

v1 whole, which is shorter than its diff:
```python
import functools

import jax
import jax.numpy as jnp
from jax import lax
from jax.experimental import pallas as pl
from jax.experimental.pallas import tpu as pltpu
from jax.sharding import PartitionSpec as P

F32 = jnp.float32
BF16 = jnp.bfloat16
TILE = 512


def dot(a, b):
    return lax.dot_general(a, b, (((1,), (0,)), ((), ())), preferred_element_type=F32)


def dot_t(a, b):
    return lax.dot_general(a, b, (((1,), (1,)), ((), ())), preferred_element_type=F32)


def kernel(
    nb, nc, nz, width,
    rhs_ref, guess_ref, inv_ref, left_ref, right_ref, ranks_ref, out_ref,
    inv, low, x, p_rhs, p_left, oc_part, oc_sum, oc_in, nc_part, nc_recv, nc_sum, nc_in,
    s_out, s_in,
    inv_sem, rhs_send, rhs_recv, left_send, left_recv, sib_send, sib_recv,
    og_send, og_recv, ob_send, ob_recv, ng_send, ng_recv, nb_send, nb_recv, rs_send, rs_recv,
):
    row, col, z = lax.axis_index("row"), lax.axis_index("col"), lax.axis_index("rhs")
    slots, part = low.shape[1:]
    m = inv.shape[2]
    rows = nz * slots
    half = col % 2
    sibling = col + 1 - 2 * half
    diag = col == z
    sent = []

    def remote(src, dst, send, recv, where):
        return pltpu.make_async_remote_copy(
            src_ref=src, dst_ref=dst, send_sem=send, recv_sem=recv,
            device_id=where, device_id_type=pl.DeviceIdType.MESH,
        )

    def start(pred, copy):
        @pl.when(pred)
        def _():
            copy.start()
        sent.append((pred, copy))

    loads = []
    for order in range(2):
        h = half if order == 0 else 1 - half
        load = pltpu.make_async_copy(
            inv_ref.at[0, pl.ds(pl.multiple_of(h * part, part), part)], inv.at[h], inv_sem.at[order]
        )
        load.start()
        loads.append(load)

    barrier = pltpu.get_barrier_semaphore()
    count = nb * nc * nz
    me = (row * nc + col) * nz + z
    for step in range(1, count):
        other = lax.rem(me + step, count)
        pl.semaphore_signal(
            barrier, inc=1,
            device_id=(other // (nc * nz), (other // nz) % nc, other % nz),
            device_id_type=pl.DeviceIdType.MESH,
        )
    for h in range(2):
        low[h] = rhs_ref[0, :, h * part:(h + 1) * part].astype(BF16)
    coef = dot_t(guess_ref[0].astype(BF16), right_ref[0].reshape(nb * width, m))
    oc_part[col] = coef
    pl.semaphore_wait(barrier, count - 1)

    mine = pl.ds(pl.multiple_of(z * slots, slots), slots)
    for c in range(nc):
        start(
            jnp.logical_not(diag & (col == c)),
            remote(low.at[c % 2], x.at[c % 2, mine], rhs_send.at[c], rhs_recv.at[z], (row, c, col)),
        )
    for q in range(nb - 1):
        block = lax.rem(row + 1 + q, nb)
        spot = pl.ds(rows + q * width, width)
        for c in range(nc):
            start(
                diag & (col != c),
                remote(
                    left_ref.at[0, block, :, pl.ds((c % 2) * part, part)],
                    x.at[c % 2, spot], left_send.at[q, c], left_recv.at[q], (row, c, z),
                ),
            )
    for step in range(1, nc):
        other = lax.rem(col + step, nc)
        start(
            row > 0,
            remote(oc_part.at[col], oc_part.at[col], og_send.at[step - 1], og_recv.at[col], (row, other, z)),
        )

    @pl.when(diag)
    def _():
        x[half, mine] = low[half]
        for q in range(nb - 1):
            block = lax.rem(row + 1 + q, nb)
            x[half, rows + q * width:rows + (q + 1) * width] = left_ref[
                0, block, :, pl.ds(pl.multiple_of(half * part, part), part)
            ]

    @pl.when(row > 0)
    def _():
        total = oc_part[col]
        for step in range(1, nc):
            other = lax.rem(col + step, nc)
            remote(
                oc_part.at[other], oc_part.at[other], og_send.at[step - 1], og_recv.at[other], (row, other, z)
            ).wait_recv()
            total = total + oc_part[other]
        lane = lax.broadcasted_iota(jnp.int32, total.shape, 1)
        kept = jnp.zeros_like(total)
        for i in range(nb):
            inside = (lane >= i * width) & (lane < i * width + ranks_ref[i, row])
            kept = jnp.where(inside, total, kept)
        oc_sum[...] = kept.astype(BF16)
    for i in range(nb - 1):
        for zz in range(nz):
            start(
                row > i,
                remote(oc_sum, oc_in.at[row, z], ob_send.at[i, zz], ob_recv.at[row, z], (i, col, zz)),
            )

    for zz in range(nz):
        @pl.when(jnp.logical_not(diag & (z == zz)))
        def _():
            spot = x.at[half, pl.ds(zz * slots, slots)]
            remote(spot, spot, rhs_send.at[0], rhs_recv.at[zz], (row, sibling, z)).wait_recv()

    @pl.when(jnp.logical_not(diag))
    def _():
        for q in range(nb - 1):
            spot = x.at[half, pl.ds(rows + q * width, width)]
            remote(spot, spot, left_send.at[0, 0], left_recv.at[q], (row, sibling, z)).wait_recv()

    swap = remote(x.at[half], x.at[half], sib_send, sib_recv, (row, sibling, z))
    swap.start()

    loads[0].wait()

    def first(i, _):
        cut = pl.ds(pl.multiple_of(i * TILE, TILE), TILE)
        value = dot(x[half], inv[half, :, cut])
        p_rhs[:, cut] = value[:rows]
        p_left[:, cut] = value[rows:]
        return _

    lax.fori_loop(0, m // TILE, first, 0)
    loads[1].wait()
    far = x.at[1 - half]
    remote(far, far, sib_send, sib_recv, (row, sibling, z)).wait_recv()

    def second(i, _):
        cut = pl.ds(pl.multiple_of(i * TILE, TILE), TILE)
        value = dot(x[1 - half], inv[1 - half, :, cut])
        p_rhs[:, cut] += value[:rows]
        p_left[:, cut] += value[rows:]
        return _

    lax.fori_loop(0, m // TILE, second, 0)
    swap.wait_send()

    fold = rows // 2
    piece = fold // nc
    for t in range(nb):
        later = nb - 1 - t
        wide = 2 * later * width

        @pl.when(row == t)
        def _():
            blocks = []
            for q in range(nb - 1):
                j = (t + 1 + q) % nb
                if j > t:
                    for zz in range(nz):
                        spot = oc_in.at[j, zz]
                        remote(spot, spot, ob_send.at[0, 0], ob_recv.at[j, zz], (j, col, zz)).wait_recv()
                    blocks.append(
                        jnp.concatenate(
                            [oc_in[j, zz][:, t * width:(t + 1) * width] for zz in range(nz)], axis=0
                        )
                    )
                else:
                    span = 2 * (nb - 1 - j) * width
                    sums = []
                    for c in range(nc):
                        total = None
                        for zz in range(nz):
                            spot = nc_in.at[j, c, zz, :, pl.ds(0, span)]
                            remote(
                                spot, spot, nb_send.at[0, 0, 0], nb_recv.at[j, c, zz], (j, c, zz)
                            ).wait_recv()
                            term = nc_in[j, c, zz, :, :span]
                            total = term if total is None else total + term
                        sums.append(total)
                    folded = jnp.concatenate(sums, axis=0)
                    at = (t - 1 - j) * width
                    whole = jnp.concatenate(
                        [folded[:, at:at + width], folded[:, span // 2 + at:span // 2 + at + width]], axis=0
                    )
                    lane = lax.broadcasted_iota(jnp.int32, whole.shape, 1)
                    whole = jnp.where(lane < ranks_ref[t, j], whole, jnp.zeros_like(whole))
                    blocks.append(whole.astype(BF16))
            coefs = blocks[0] if nb == 2 else jnp.concatenate(blocks, axis=1)
            p_rhs[...] = p_rhs[...] - dot(coefs, p_left[...].astype(BF16))
            for zz in range(nz):
                s_out[zz] = p_rhs[zz * slots:(zz + 1) * slots].astype(BF16)
            if later:
                value = dot_t(
                    s_out[...].reshape(rows, m), right_ref[0, t + 1:].reshape(later * width, m)
                )
                folded = jnp.concatenate([value[:fold], value[fold:]], axis=1)
                for c in range(nc):
                    nc_part[c, :, :wide] = folded[c * piece:(c + 1) * piece]

        if later:
            for step in range(1, nc):
                other = lax.rem(col + step, nc)
                start(
                    row == t,
                    remote(
                        nc_part.at[other, :, pl.ds(0, wide)], nc_recv.at[col, :, pl.ds(0, wide)],
                        ng_send.at[step - 1], ng_recv.at[col], (row, other, z),
                    ),
                )
        for step in range(1, nz):
            other = lax.rem(z + step, nz)
            start(
                row == t,
                remote(s_out.at[other], s_in.at[z], rs_send.at[step - 1], rs_recv.at[z], (row, col, other)),
            )
        if later:
            @pl.when(row == t)
            def _():
                total = nc_part[col, :, :wide]
                for step in range(1, nc):
                    other = lax.rem(col + step, nc)
                    spot = nc_recv.at[other, :, pl.ds(0, wide)]
                    remote(spot, spot, ng_send.at[0], ng_recv.at[other], (row, other, z)).wait_recv()
                    total = total + nc_recv[other, :, :wide]
                nc_sum[:, :wide] = total
            for i in range(t + 1, nb):
                for c in range(nc):
                    for zz in range(nz):
                        start(
                            row == t,
                            remote(
                                nc_sum.at[:, pl.ds(0, wide)], nc_in.at[t, col, z, :, pl.ds(0, wide)],
                                nb_send.at[i, c, zz], nb_recv.at[t, col, z], (i, c, zz),
                            ),
                        )

    total = p_rhs[mine]
    for step in range(1, nz):
        other = lax.rem(z + step, nz)
        spot = s_in.at[other]
        remote(spot, spot, rs_send.at[0], rs_recv.at[other], (row, col, other)).wait_recv()
        total = total + s_in[other].astype(F32)
    out_ref[0] = total
    for pred, copy in sent:
        @pl.when(pred)
        def _():
            copy.wait_send()


def solution(mesh):
    nb, nc, nz = mesh.shape["row"], mesh.shape["col"], mesh.shape["rhs"]

    def body(right_side, guess, inverse, left_factor, right_factor, ranks):
        slots, m = right_side.shape[1:]
        width = left_factor.shape[2]
        rows = nz * slots
        part = inverse.shape[1] // 2
        deep = rows + (nb - 1) * width
        piece = rows // 2 // nc
        wide = 2 * (nb - 1) * width
        dma = pltpu.SemaphoreType.DMA
        vmem = pl.BlockSpec(memory_space=pltpu.VMEM)
        return pl.pallas_call(
            functools.partial(kernel, nb, nc, nz, width),
            out_shape=jax.ShapeDtypeStruct(right_side.shape, F32),
            in_specs=[
                vmem, vmem, pl.BlockSpec(memory_space=pltpu.HBM), vmem, vmem,
                pl.BlockSpec(memory_space=pltpu.SMEM),
            ],
            out_specs=vmem,
            scratch_shapes=[
                pltpu.VMEM((2, part, m), BF16),
                pltpu.VMEM((2, slots, part), BF16),
                pltpu.VMEM((2, deep, part), BF16),
                pltpu.VMEM((rows, m), F32),
                pltpu.VMEM((deep - rows, m), F32),
                pltpu.VMEM((nc, slots, nb * width), F32),
                pltpu.VMEM((slots, nb * width), BF16),
                pltpu.VMEM((nb, nz, slots, nb * width), BF16),
                pltpu.VMEM((nc, piece, wide), F32),
                pltpu.VMEM((nc, piece, wide), F32),
                pltpu.VMEM((piece, wide), F32),
                pltpu.VMEM((nb, nc, nz, piece, wide), F32),
                pltpu.VMEM((nz, slots, m), BF16),
                pltpu.VMEM((nz, slots, m), BF16),
                dma((2,)),
                dma((nc,)), dma((nz,)),
                dma((nb - 1, nc)), dma((nb - 1,)),
                dma, dma,
                dma((nc - 1,)), dma((nc,)),
                dma((nb - 1, nz)), dma((nb, nz)),
                dma((nc - 1,)), dma((nc,)),
                dma((nb, nc, nz)), dma((nb, nc, nz)),
                dma((nz - 1,)), dma((nz,)),
            ],
            compiler_params=pltpu.CompilerParams(
                collective_id=0, has_side_effects=True, vmem_limit_bytes=60 * 1024 * 1024
            ),
        )(right_side, guess, inverse, left_factor, right_factor, ranks)

    in_specs = (
        P("row", "rhs", "col"),
        P("row", "rhs", "col"),
        P("row", "rhs", "col"),
        P("row", None, None, "col"),
        P("row", None, None, "col"),
        P(),
    )
    out_specs = P("row", "rhs", "col")
    return jax.shard_map(body, mesh=mesh, in_specs=in_specs, out_specs=out_specs, check_vma=False)
```

time: 151 us -> 37.8 us (0.25)
  blocking collectives: 71.3 us -> 0 us
  waiting for transfers between devices: 42.4 us -> 0 us
  Pallas kernels: 0 us -> 36.1 us
  matrix products: 15.5 us -> 0 us
  between operations: 13.4 us -> 0.01 us
  starting transfers between devices: 3.79 us -> 0 us
  other arithmetic: 1.65 us -> 0 us
    reduce_scatter x2 -> x0, waiting for transfers between devices: 40.6 us -> none  [body(): current = lax.psum_scatter(product, 'rhs', scatter_dimension=0, tiled=True)]
    pallas_call x0 -> x1, Pallas kernels: none -> 36.1 us  [body(): pl.pallas_call(functools.partial(kernel, nb, nc, nz, width), out_shape=ja...]
    psum x2 -> x0, blocking collectives: 33.6 us -> none  [the longest x1 22.4 us: body(): shared = lax.psum(coef, ('row', 'col')).astype(jnp.bfloat16)]
    all_to_all x2 -> x0, blocking collectives: 26.1 us -> none  [body(): lax.all_to_all(residue_full, 'rhs', split_axis=1, concat_axis=0, tiled=True)]
    dot_general x6 -> x0, matrix products: 15.5 us -> none  [the longest x2 11.6 us: body(): product = jnp.dot(pieces, inverse[0], preferred_element_type=jnp.float32)]
    all_gather x2 -> x0, blocking collectives: 11.6 us -> none  [body(): residue_full = lax.all_gather(residue, 'col', axis=1, tiled=True)]
    all_to_all x1 -> x0, starting transfers between devices: 3.74 us -> none  [body(): lax.all_to_all(old_sum, 'row', split_axis=0, concat_axis=0, tiled=True)]
    all_to_all x1 -> x0, waiting for transfers between devices: 1.77 us -> none  [body(): lax.all_to_all(old_sum, 'row', split_axis=0, concat_axis=0, tiled=True)]
  transfers between devices with their start and end apart: 3 -> 0, of which waited for: 3 -> 0; matrix products, arithmetic and copies ran while one was open for 0% -> 0% of each run, Pallas kernels for 0% -> 0%
where the time goes in v1:
time: 37.8 us; the launch traced here: 37.7 us
  Pallas kernels  36.1 us (96%)
  local copies, waits for them, and re-layouts  1.57 us (4%)
    pallas_call x1, Pallas kernels, body(): pl.pallas_call(functools.partial(kernel, nb, nc, nz, width), out_shape=ja...  36.1 us
    unnamed x1, local copies, waits for them, and re-layouts  1.57 us

profile of v1, /device:TPU:2, one launch (start us, length us, event | category | flops | bytes accessed | tf_op | source)
XLA Modules:
  0.0 37.7 jit_solution(7139686106757325268)
XLA Ops:
  0.0 36.1 %shard_map.64 = f32[1,16,2048]{2,1,0:T(8,128)} custom-call(f32[1,16,2048]{2,1,0:T(8,128)} %rhs_ref.1, f32[1,16,2048]{2,1,0:T(8,128)} %guess_ref.1, bf16[1,2048,2048]{2,1,0:T(8,128)(2,1)} %inv_ref.1, bf16[1,2,64,2048]{3,2,1,0:T(8,128)(2,1)} %left_ref.1, bf16[1,2,64,2048]{3,2,1,0:T(8,128)(2,1)} %right_ref.1, s32[2,2]{1,0:T(2,128)} %ranks_ref.1), custom_call_target="tpu_custom_call" | custom-call | tf_op jit(solution)/shard_map/pallas_call | solution.py:287
  36.1 1.6 %copy.8 = f32[1,16,2048]{2,1,0:T(8,128)} copy(f32[1,16,2048]{2,1,0:T(8,128)} %shard_map.64) | data formatting | bytes 262144

commit v2 on v1

--- a/solution.py
+++ b/solution.py
@@ -10,6 +10,7 @@
 F32 = jnp.float32
 BF16 = jnp.bfloat16
 TILE = 512
+CHUNKS = 4
 
 
 def dot(a, b):
@@ -23,9 +24,9 @@
 def kernel(
     nb, nc, nz, width,
     rhs_ref, guess_ref, inv_ref, left_ref, right_ref, ranks_ref, out_ref,
-    inv, low, x, p_rhs, p_left, oc_part, oc_sum, oc_in, nc_part, nc_recv, nc_sum, nc_in,
+    inv, rhs_v, guess_v, right_v, low, x, p_rhs, p_left, p_low, oc_part, oc_sum, oc_in, nc_part, nc_recv, nc_sum, nc_in,
     s_out, s_in,
-    inv_sem, rhs_send, rhs_recv, left_send, left_recv, sib_send, sib_recv,
+    inv_sem, in_sem, own_sem, rhs_send, rhs_recv, left_send, left_recv, sib_send, sib_recv,
     og_send, og_recv, ob_send, ob_recv, ng_send, ng_recv, nb_send, nb_recv, rs_send, rs_recv,
 ):
     row, col, z = lax.axis_index("row"), lax.axis_index("col"), lax.axis_index("rhs")
@@ -49,15 +50,6 @@
             copy.start()
         sent.append((pred, copy))
 
-    loads = []
-    for order in range(2):
-        h = half if order == 0 else 1 - half
-        load = pltpu.make_async_copy(
-            inv_ref.at[0, pl.ds(pl.multiple_of(h * part, part), part)], inv.at[h], inv_sem.at[order]
-        )
-        load.start()
-        loads.append(load)
-
     barrier = pltpu.get_barrier_semaphore()
     count = nb * nc * nz
     me = (row * nc + col) * nz + z
@@ -68,11 +60,38 @@
             device_id=(other // (nc * nz), (other // nz) % nc, other % nz),
             device_id_type=pl.DeviceIdType.MESH,
         )
+    early = [
+        pltpu.make_async_copy(src, dst, in_sem.at[i])
+        for i, (src, dst) in enumerate(
+            ((rhs_ref.at[0], rhs_v), (guess_ref.at[0], guess_v), (right_ref.at[0], right_v))
+        )
+    ]
+    for load in early:
+        load.start()
+    loads = []
+    for order in range(2):
+        h = half if order == 0 else 1 - half
+        load = pltpu.make_async_copy(
+            inv_ref.at[0, pl.ds(pl.multiple_of(h * part, part), part)], inv.at[h], inv_sem.at[order]
+        )
+        load.start()
+        loads.append(load)
+
+    early[0].wait()
     for h in range(2):
-        low[h] = rhs_ref[0, :, h * part:(h + 1) * part].astype(BF16)
-    coef = dot_t(guess_ref[0].astype(BF16), right_ref[0].reshape(nb * width, m))
+        low[h] = rhs_v[:, h * part:(h + 1) * part].astype(BF16)
+    early[1].wait()
+    early[2].wait()
+    coef = dot_t(guess_v[...].astype(BF16), right_v[...].reshape(nb * width, m))
     oc_part[col] = coef
     pl.semaphore_wait(barrier, count - 1)
+
+    for step in range(1, nc):
+        other = lax.rem(col + step, nc)
+        start(
+            row > 0,
+            remote(oc_part.at[col], oc_part.at[col], og_send.at[step - 1], og_recv.at[col], (row, other, z)),
+        )
 
     mine = pl.ds(pl.multiple_of(z * slots, slots), slots)
     for c in range(nc):
@@ -91,21 +110,17 @@
                     x.at[c % 2, spot], left_send.at[q, c], left_recv.at[q], (row, c, z),
                 ),
             )
-    for step in range(1, nc):
-        other = lax.rem(col + step, nc)
-        start(
-            row > 0,
-            remote(oc_part.at[col], oc_part.at[col], og_send.at[step - 1], og_recv.at[col], (row, other, z)),
+    def own(q):
+        return pltpu.make_async_copy(
+            left_ref.at[0, lax.rem(row + 1 + q, nb), :, pl.ds(pl.multiple_of(half * part, part), part)],
+            x.at[half, pl.ds(rows + q * width, width)], own_sem.at[q],
         )
 
     @pl.when(diag)
     def _():
+        for q in range(nb - 1):
+            own(q).start()
         x[half, mine] = low[half]
-        for q in range(nb - 1):
-            block = lax.rem(row + 1 + q, nb)
-            x[half, rows + q * width:rows + (q + 1) * width] = left_ref[
-                0, block, :, pl.ds(pl.multiple_of(half * part, part), part)
-            ]
 
     @pl.when(row > 0)
     def _():
@@ -135,6 +150,11 @@
             spot = x.at[half, pl.ds(zz * slots, slots)]
             remote(spot, spot, rhs_send.at[0], rhs_recv.at[zz], (row, sibling, z)).wait_recv()
 
+    @pl.when(diag)
+    def _():
+        for q in range(nb - 1):
+            own(q).wait()
+
     @pl.when(jnp.logical_not(diag))
     def _():
         for q in range(nb - 1):
@@ -162,7 +182,7 @@
         cut = pl.ds(pl.multiple_of(i * TILE, TILE), TILE)
         value = dot(x[1 - half], inv[1 - half, :, cut])
         p_rhs[:, cut] += value[:rows]
-        p_left[:, cut] += value[rows:]
+        p_low[:, cut] = (p_left[:, cut] + value[rows:]).astype(BF16)
         return _
 
     lax.fori_loop(0, m // TILE, second, 0)
@@ -170,6 +190,21 @@
 
     fold = rows // 2
     piece = fold // nc
+    span_m = m // CHUNKS
+    others = [lax.rem(z + step, nz) for step in range(1, nz)]
+
+    def pieces(ch):
+        return [
+            remote(
+                s_out.at[ch, other], s_in.at[ch, z], rs_send.at[ch, i], rs_recv.at[ch, z], (row, col, other)
+            )
+            for i, other in enumerate(others)
+        ]
+
+    def scatter(t, ch):
+        for copy in pieces(ch):
+            copy.start()
+
     for t in range(nb):
         later = nb - 1 - t
         wide = 2 * later * width
@@ -210,13 +245,20 @@
                     whole = jnp.where(lane < ranks_ref[t, j], whole, jnp.zeros_like(whole))
                     blocks.append(whole.astype(BF16))
             coefs = blocks[0] if nb == 2 else jnp.concatenate(blocks, axis=1)
-            p_rhs[...] = p_rhs[...] - dot(coefs, p_left[...].astype(BF16))
-            for zz in range(nz):
-                s_out[zz] = p_rhs[zz * slots:(zz + 1) * slots].astype(BF16)
+            value = None
+            for ch in range(CHUNKS):
+                cut = slice(ch * span_m, (ch + 1) * span_m)
+                now = p_rhs[:, cut] - dot(coefs, p_low[:, cut])
+                p_rhs[:, cut] = now
+                now = now.astype(BF16)
+                for zz in range(nz):
+                    s_out[ch, zz] = now[zz * slots:(zz + 1) * slots]
+                if later:
+                    term = dot_t(now, right_v[t + 1:, :, cut].reshape(later * width, span_m))
+                    value = term if value is None else value + term
+                else:
+                    scatter(t, ch)
             if later:
-                value = dot_t(
-                    s_out[...].reshape(rows, m), right_ref[0, t + 1:].reshape(later * width, m)
-                )
                 folded = jnp.concatenate([value[:fold], value[fold:]], axis=1)
                 for c in range(nc):
                     nc_part[c, :, :wide] = folded[c * piece:(c + 1) * piece]
@@ -231,12 +273,6 @@
                         ng_send.at[step - 1], ng_recv.at[col], (row, other, z),
                     ),
                 )
-        for step in range(1, nz):
-            other = lax.rem(z + step, nz)
-            start(
-                row == t,
-                remote(s_out.at[other], s_in.at[z], rs_send.at[step - 1], rs_recv.at[z], (row, col, other)),
-            )
         if later:
             @pl.when(row == t)
             def _():
@@ -258,13 +294,22 @@
                             ),
                         )
 
-    total = p_rhs[mine]
-    for step in range(1, nz):
-        other = lax.rem(z + step, nz)
-        spot = s_in.at[other]
-        remote(spot, spot, rs_send.at[0], rs_recv.at[other], (row, col, other)).wait_recv()
-        total = total + s_in[other].astype(F32)
-    out_ref[0] = total
+            @pl.when(row == t)
+            def _():
+                for ch in range(CHUNKS):
+                    scatter(t, ch)
+
+    for ch in range(CHUNKS):
+        cut = slice(ch * span_m, (ch + 1) * span_m)
+        total = p_rhs[mine, cut]
+        for other in others:
+            spot = s_in.at[ch, other]
+            remote(spot, spot, rs_send.at[0, 0], rs_recv.at[ch, other], (row, col, other)).wait_recv()
+            total = total + s_in[ch, other].astype(F32)
+        out_ref[0, :, cut] = total
+    for ch in range(CHUNKS):
+        for copy in pieces(ch):
+            copy.wait_send()
     for pred, copy in sent:
         @pl.when(pred)
         def _():
@@ -283,21 +328,26 @@
         piece = rows // 2 // nc
         wide = 2 * (nb - 1) * width
         dma = pltpu.SemaphoreType.DMA
+        hbm = pl.BlockSpec(memory_space=pltpu.HBM)
         vmem = pl.BlockSpec(memory_space=pltpu.VMEM)
         return pl.pallas_call(
             functools.partial(kernel, nb, nc, nz, width),
             out_shape=jax.ShapeDtypeStruct(right_side.shape, F32),
             in_specs=[
-                vmem, vmem, pl.BlockSpec(memory_space=pltpu.HBM), vmem, vmem,
+                hbm, hbm, hbm, hbm, hbm,
                 pl.BlockSpec(memory_space=pltpu.SMEM),
             ],
             out_specs=vmem,
             scratch_shapes=[
                 pltpu.VMEM((2, part, m), BF16),
+                pltpu.VMEM((slots, m), F32),
+                pltpu.VMEM((slots, m), F32),
+                pltpu.VMEM((nb, width, m), BF16),
                 pltpu.VMEM((2, slots, part), BF16),
                 pltpu.VMEM((2, deep, part), BF16),
                 pltpu.VMEM((rows, m), F32),
                 pltpu.VMEM((deep - rows, m), F32),
+                pltpu.VMEM((deep - rows, m), BF16),
                 pltpu.VMEM((nc, slots, nb * width), F32),
                 pltpu.VMEM((slots, nb * width), BF16),
                 pltpu.VMEM((nb, nz, slots, nb * width), BF16),
@@ -305,9 +355,9 @@
                 pltpu.VMEM((nc, piece, wide), F32),
                 pltpu.VMEM((piece, wide), F32),
                 pltpu.VMEM((nb, nc, nz, piece, wide), F32),
-                pltpu.VMEM((nz, slots, m), BF16),
-                pltpu.VMEM((nz, slots, m), BF16),
-                dma((2,)),
+                pltpu.VMEM((CHUNKS, nz, slots, m // CHUNKS), BF16),
+                pltpu.VMEM((CHUNKS, nz, slots, m // CHUNKS), BF16),
+                dma((2,)), dma((3,)), dma((nb - 1,)),
                 dma((nc,)), dma((nz,)),
                 dma((nb - 1, nc)), dma((nb - 1,)),
                 dma, dma,
@@ -315,7 +365,7 @@
                 dma((nb - 1, nz)), dma((nb, nz)),
                 dma((nc - 1,)), dma((nc,)),
                 dma((nb, nc, nz)), dma((nb, nc, nz)),
-                dma((nz - 1,)), dma((nz,)),
+                dma((CHUNKS, nz - 1)), dma((CHUNKS, nz)),
             ],
             compiler_params=pltpu.CompilerParams(
                 collective_id=0, has_side_effects=True, vmem_limit_bytes=60 * 1024 * 1024

time: 37.8 us -> 35.1 us (0.929); the launches traced: 37.7 us -> 34.5 us
  Pallas kernels: 36.1 us -> 32.9 us
    pallas_call x1, Pallas kernels: 36.1 us -> 32.9 us  [body(): pl.pallas_call(functools.partial(kernel, nb, nc, nz, width), out_shape=ja...]
where the time goes in v2:
time: 35.1 us; the launch traced here: 34.5 us
  Pallas kernels  32.9 us (94%)
  local copies, waits for them, and re-layouts  1.57 us (4%)
    pallas_call x1, Pallas kernels, body(): pl.pallas_call(functools.partial(kernel, nb, nc, nz, width), out_shape=ja...  32.9 us
    unnamed x1, local copies, waits for them, and re-layouts  1.57 us

profile of v2, /device:TPU:2, one launch (start us, length us, event | category | flops | bytes accessed | tf_op | source)
XLA Modules:
  0.0 34.5 jit_solution(1712955052643451234)
XLA Ops:
  0.0 32.9 %shard_map.64 = f32[1,16,2048]{2,1,0:T(8,128)} custom-call(f32[1,16,2048]{2,1,0:T(8,128)} %rhs_ref.1, f32[1,16,2048]{2,1,0:T(8,128)} %guess_ref.1, bf16[1,2048,2048]{2,1,0:T(8,128)(2,1)} %inv_ref.1, bf16[1,2,64,2048]{3,2,1,0:T(8,128)(2,1)} %left_ref.1, bf16[1,2,64,2048]{3,2,1,0:T(8,128)(2,1)} %right_ref.1, s32[2,2]{1,0:T(2,128)} %ranks_ref.1), custom_call_target="tpu_custom_call" | custom-call | tf_op jit(solution)/shard_map/pallas_call | solution.py:333
  32.9 1.6 %copy.8 = f32[1,16,2048]{2,1,0:T(8,128)} copy(f32[1,16,2048]{2,1,0:T(8,128)} %shard_map.64) | data formatting | bytes 262144

commit v3 on v2

--- a/solution.py
+++ b/solution.py
@@ -24,10 +24,12 @@
 def kernel(
     nb, nc, nz, width,
     rhs_ref, guess_ref, inv_ref, left_ref, right_ref, ranks_ref, out_ref,
-    inv, rhs_v, guess_v, right_v, low, x, p_rhs, p_left, p_low, oc_part, oc_sum, oc_in, nc_part, nc_recv, nc_sum, nc_in,
+    inv, rhs_v, guess_v, right_v, low, x, p_rhs, p_left, p_low, p_sum, w_in,
+    coef_v, f_out, f_in, oc_part, oc_sum, oc_in, nc_part, nc_recv, nc_sum, nc_in,
     s_out, s_in,
     inv_sem, in_sem, own_sem, rhs_send, rhs_recv, left_send, left_recv, sib_send, sib_recv,
     og_send, og_recv, ob_send, ob_recv, ng_send, ng_recv, nb_send, nb_recv, rs_send, rs_recv,
+    w_send, w_recv, f_send, f_recv,
 ):
     row, col, z = lax.axis_index("row"), lax.axis_index("col"), lax.axis_index("rhs")
     slots, part = low.shape[1:]
@@ -178,18 +180,6 @@
     far = x.at[1 - half]
     remote(far, far, sib_send, sib_recv, (row, sibling, z)).wait_recv()
 
-    def second(i, _):
-        cut = pl.ds(pl.multiple_of(i * TILE, TILE), TILE)
-        value = dot(x[1 - half], inv[1 - half, :, cut])
-        p_rhs[:, cut] += value[:rows]
-        p_low[:, cut] = (p_left[:, cut] + value[rows:]).astype(BF16)
-        return _
-
-    lax.fori_loop(0, m // TILE, second, 0)
-    swap.wait_send()
-
-    fold = rows // 2
-    piece = fold // nc
     span_m = m // CHUNKS
     others = [lax.rem(z + step, nz) for step in range(1, nz)]
 
@@ -201,16 +191,52 @@
             for i, other in enumerate(others)
         ]
 
-    def scatter(t, ch):
+    def scatter(ch):
         for copy in pieces(ch):
             copy.start()
 
+    def keep(ch, now):
+        for zz in range(nz):
+            s_out[ch, zz] = now[zz * slots:(zz + 1) * slots]
+
+    partner = z + 1 - 2 * (z % 2)
+    pairs = nz // 2
+
+    def paired(ch):
+        cut = pl.ds(ch * span_m, span_m)
+        return remote(p_low.at[:, cut], w_in.at[:, cut], w_send.at[ch], w_recv.at[ch], (row, col, partner))
+
+    for ch in range(CHUNKS):
+        cut = slice(ch * span_m, (ch + 1) * span_m)
+        value = dot(x[1 - half], inv[1 - half, :, cut])
+        now = p_rhs[:, cut] + value[:rows]
+        p_rhs[:, cut] = now
+        p_low[:, cut] = (p_left[:, cut] + value[rows:]).astype(BF16)
+
+        @pl.when(row > 0)
+        def _():
+            paired(ch).start()
+            keep(ch, now.astype(BF16))
+
+    @pl.when(row > 0)
+    def _():
+        for ch in range(CHUNKS):
+            scatter(ch)
+    swap.wait_send()
+
+    fold = rows // 2
+    piece = fold // nc
     for t in range(nb):
         later = nb - 1 - t
         wide = 2 * later * width
 
         @pl.when(row == t)
         def _():
+            if t > 0:
+                for ch in range(CHUNKS):
+                    cut = slice(ch * span_m, (ch + 1) * span_m)
+                    paired(ch).wait_recv()
+                    p_sum[:, cut] = (p_low[:, cut].astype(F32) + w_in[:, cut].astype(F32)).astype(BF16)
             blocks = []
             for q in range(nb - 1):
                 j = (t + 1 + q) % nb
@@ -246,18 +272,20 @@
                     blocks.append(whole.astype(BF16))
             coefs = blocks[0] if nb == 2 else jnp.concatenate(blocks, axis=1)
             value = None
-            for ch in range(CHUNKS):
-                cut = slice(ch * span_m, (ch + 1) * span_m)
-                now = p_rhs[:, cut] - dot(coefs, p_low[:, cut])
-                p_rhs[:, cut] = now
-                now = now.astype(BF16)
-                for zz in range(nz):
-                    s_out[ch, zz] = now[zz * slots:(zz + 1) * slots]
-                if later:
-                    term = dot_t(now, right_v[t + 1:, :, cut].reshape(later * width, span_m))
-                    value = term if value is None else value + term
-                else:
-                    scatter(t, ch)
+            if t == 0 or later:
+                for ch in range(CHUNKS):
+                    cut = slice(ch * span_m, (ch + 1) * span_m)
+                    now = p_rhs[:, cut] - dot(coefs, p_low[:, cut])
+                    if t == 0:
+                        p_rhs[:, cut] = now
+                    now = now.astype(BF16)
+                    if t == 0:
+                        keep(ch, now)
+                    if later:
+                        term = dot_t(now, right_v[t + 1:, :, cut].reshape(later * width, span_m))
+                        value = term if value is None else value + term
+            if t > 0:
+                coef_v[...] = coefs
             if later:
                 folded = jnp.concatenate([value[:fold], value[fold:]], axis=1)
                 for c in range(nc):
@@ -294,10 +322,38 @@
                             ),
                         )
 
-            @pl.when(row == t)
-            def _():
-                for ch in range(CHUNKS):
-                    scatter(t, ch)
+
+    @pl.when(row == 0)
+    def _():
+        for ch in range(CHUNKS):
+            scatter(ch)
+
+    @pl.when(row > 0)
+    def _():
+        spots = [lax.rem(z + 2 * k, nz) for k in range(pairs)]
+        picked = jnp.concatenate(
+            [coef_v[pl.ds(pl.multiple_of(spot * slots, slots), slots)] for spot in spots], axis=0
+        )
+
+        def across(k, ch):
+            return remote(
+                f_out.at[k - 1, ch], f_in.at[k - 1, ch], f_send.at[k - 1, ch], f_recv.at[k - 1, ch],
+                (row, col, spots[k]),
+            )
+
+        for ch in range(CHUNKS):
+            cut = slice(ch * span_m, (ch + 1) * span_m)
+            value = dot(picked, p_sum[:, cut])
+            for k in range(1, pairs):
+                f_out[k - 1, ch] = value[k * slots:(k + 1) * slots].astype(BF16)
+                across(k, ch).start()
+            p_rhs[mine, cut] = p_rhs[mine, cut] - value[:slots]
+        for ch in range(CHUNKS):
+            cut = slice(ch * span_m, (ch + 1) * span_m)
+            for k in range(1, pairs):
+                across(k, ch).wait()
+                p_rhs[mine, cut] = p_rhs[mine, cut] - f_in[k - 1, ch].astype(F32)
+            paired(ch).wait_send()
 
     for ch in range(CHUNKS):
         cut = slice(ch * span_m, (ch + 1) * span_m)
@@ -348,6 +404,11 @@
                 pltpu.VMEM((rows, m), F32),
                 pltpu.VMEM((deep - rows, m), F32),
                 pltpu.VMEM((deep - rows, m), BF16),
+                pltpu.VMEM((deep - rows, m), BF16),
+                pltpu.VMEM((deep - rows, m), BF16),
+                pltpu.VMEM((rows, deep - rows), BF16),
+                pltpu.VMEM((nz // 2 - 1, CHUNKS, slots, m // CHUNKS), BF16),
+                pltpu.VMEM((nz // 2 - 1, CHUNKS, slots, m // CHUNKS), BF16),
                 pltpu.VMEM((nc, slots, nb * width), F32),
                 pltpu.VMEM((slots, nb * width), BF16),
                 pltpu.VMEM((nb, nz, slots, nb * width), BF16),
@@ -366,6 +427,8 @@
                 dma((nc - 1,)), dma((nc,)),
                 dma((nb, nc, nz)), dma((nb, nc, nz)),
                 dma((CHUNKS, nz - 1)), dma((CHUNKS, nz)),
+                dma((CHUNKS,)), dma((CHUNKS,)),
+                dma((nz // 2 - 1, CHUNKS)), dma((nz // 2 - 1, CHUNKS)),
             ],
             compiler_params=pltpu.CompilerParams(
                 collective_id=0, has_side_effects=True, vmem_limit_bytes=60 * 1024 * 1024

time: 35.1 us -> 33.6 us (0.957); the launches traced: 34.5 us -> 33.4 us
  Pallas kernels: 32.9 us -> 31.9 us
    pallas_call x1, Pallas kernels: 32.9 us -> 31.9 us  [body(): pl.pallas_call(functools.partial(kernel, nb, nc, nz, width), out_shape=ja...]
where the time goes in v3:
time: 33.6 us; the launch traced here: 33.4 us
  Pallas kernels  31.9 us (95%)
  local copies, waits for them, and re-layouts  1.57 us (5%)
    pallas_call x1, Pallas kernels, body(): pl.pallas_call(functools.partial(kernel, nb, nc, nz, width), out_shape=ja...  31.9 us
    unnamed x1, local copies, waits for them, and re-layouts  1.57 us

profile of v3, /device:TPU:2, one launch (start us, length us, event | category | flops | bytes accessed | tf_op | source)
XLA Modules:
  0.0 33.4 jit_solution(10090272590901315089)
XLA Ops:
  0.0 31.9 %shard_map.64 = f32[1,16,2048]{2,1,0:T(8,128)} custom-call(f32[1,16,2048]{2,1,0:T(8,128)} %rhs_ref.1, f32[1,16,2048]{2,1,0:T(8,128)} %guess_ref.1, bf16[1,2048,2048]{2,1,0:T(8,128)(2,1)} %inv_ref.1, bf16[1,2,64,2048]{3,2,1,0:T(8,128)(2,1)} %left_ref.1, bf16[1,2,64,2048]{3,2,1,0:T(8,128)(2,1)} %right_ref.1, s32[2,2]{1,0:T(2,128)} %ranks_ref.1), custom_call_target="tpu_custom_call" | custom-call | tf_op jit(solution)/shard_map/pallas_call | solution.py:389
  31.9 1.6 %copy.8 = f32[1,16,2048]{2,1,0:T(8,128)} copy(f32[1,16,2048]{2,1,0:T(8,128)} %shard_map.64) | data formatting | bytes 262144

commit v4 on v3

--- a/solution.py
+++ b/solution.py
@@ -10,7 +10,7 @@
 F32 = jnp.float32
 BF16 = jnp.bfloat16
 TILE = 512
-CHUNKS = 4
+CHUNKS = 2
 
 
 def dot(a, b):
@@ -53,15 +53,11 @@
         sent.append((pred, copy))
 
     barrier = pltpu.get_barrier_semaphore()
-    count = nb * nc * nz
-    me = (row * nc + col) * nz + z
-    for step in range(1, count):
-        other = lax.rem(me + step, count)
-        pl.semaphore_signal(
-            barrier, inc=1,
-            device_id=(other // (nc * nz), (other // nz) % nc, other % nz),
-            device_id_type=pl.DeviceIdType.MESH,
-        )
+    peers = [
+        (row, lax.rem(col + dc, nc), lax.rem(z + dz, nz)) for dc in range(nc) for dz in range(nz) if dc or dz
+    ] + [(lax.rem(row + dr, nb), col, lax.rem(z + dz, nz)) for dr in range(1, nb) for dz in range(nz)]
+    for peer in peers:
+        pl.semaphore_signal(barrier, inc=1, device_id=peer, device_id_type=pl.DeviceIdType.MESH)
     early = [
         pltpu.make_async_copy(src, dst, in_sem.at[i])
         for i, (src, dst) in enumerate(
@@ -86,7 +82,7 @@
     early[2].wait()
     coef = dot_t(guess_v[...].astype(BF16), right_v[...].reshape(nb * width, m))
     oc_part[col] = coef
-    pl.semaphore_wait(barrier, count - 1)
+    pl.semaphore_wait(barrier, len(peers))
 
     for step in range(1, nc):
         other = lax.rem(col + step, nc)
@@ -225,7 +221,6 @@
     swap.wait_send()
 
     fold = rows // 2
-    piece = fold // nc
     for t in range(nb):
         later = nb - 1 - t
         wide = 2 * later * width
@@ -251,18 +246,12 @@
                     )
                 else:
                     span = 2 * (nb - 1 - j) * width
-                    sums = []
-                    for c in range(nc):
-                        total = None
-                        for zz in range(nz):
-                            spot = nc_in.at[j, c, zz, :, pl.ds(0, span)]
-                            remote(
-                                spot, spot, nb_send.at[0, 0, 0], nb_recv.at[j, c, zz], (j, c, zz)
-                            ).wait_recv()
-                            term = nc_in[j, c, zz, :, :span]
-                            total = term if total is None else total + term
-                        sums.append(total)
-                    folded = jnp.concatenate(sums, axis=0)
+                    folded = None
+                    for zz in range(nz):
+                        spot = nc_in.at[j, zz, :, pl.ds(0, span)]
+                        remote(spot, spot, nb_send.at[0, 0], nb_recv.at[j, zz], (j, col, zz)).wait_recv()
+                        term = nc_in[j, zz, :, :span]
+                        folded = term if folded is None else folded + term
                     at = (t - 1 - j) * width
                     whole = jnp.concatenate(
                         [folded[:, at:at + width], folded[:, span // 2 + at:span // 2 + at + width]], axis=0
@@ -288,8 +277,7 @@
                 coef_v[...] = coefs
             if later:
                 folded = jnp.concatenate([value[:fold], value[fold:]], axis=1)
-                for c in range(nc):
-                    nc_part[c, :, :wide] = folded[c * piece:(c + 1) * piece]
+                nc_part[:, :wide] = folded
 
         if later:
             for step in range(1, nc):
@@ -297,14 +285,14 @@
                 start(
                     row == t,
                     remote(
-                        nc_part.at[other, :, pl.ds(0, wide)], nc_recv.at[col, :, pl.ds(0, wide)],
+                        nc_part.at[:, pl.ds(0, wide)], nc_recv.at[col, :, pl.ds(0, wide)],
                         ng_send.at[step - 1], ng_recv.at[col], (row, other, z),
                     ),
                 )
         if later:
             @pl.when(row == t)
             def _():
-                total = nc_part[col, :, :wide]
+                total = nc_part[:, :wide]
                 for step in range(1, nc):
                     other = lax.rem(col + step, nc)
                     spot = nc_recv.at[other, :, pl.ds(0, wide)]
@@ -312,16 +300,14 @@
                     total = total + nc_recv[other, :, :wide]
                 nc_sum[:, :wide] = total
             for i in range(t + 1, nb):
-                for c in range(nc):
-                    for zz in range(nz):
-                        start(
-                            row == t,
-                            remote(
-                                nc_sum.at[:, pl.ds(0, wide)], nc_in.at[t, col, z, :, pl.ds(0, wide)],
-                                nb_send.at[i, c, zz], nb_recv.at[t, col, z], (i, c, zz),
-                            ),
-                        )
-
+                for zz in range(nz):
+                    start(
+                        row == t,
+                        remote(
+                            nc_sum.at[:, pl.ds(0, wide)], nc_in.at[t, z, :, pl.ds(0, wide)],
+                            nb_send.at[i, zz], nb_recv.at[t, z], (i, col, zz),
+                        ),
+                    )
 
     @pl.when(row == 0)
     def _():
@@ -381,7 +367,6 @@
         rows = nz * slots
         part = inverse.shape[1] // 2
         deep = rows + (nb - 1) * width
-        piece = rows // 2 // nc
         wide = 2 * (nb - 1) * width
         dma = pltpu.SemaphoreType.DMA
         hbm = pl.BlockSpec(memory_space=pltpu.HBM)
@@ -412,10 +397,10 @@
                 pltpu.VMEM((nc, slots, nb * width), F32),
                 pltpu.VMEM((slots, nb * width), BF16),
                 pltpu.VMEM((nb, nz, slots, nb * width), BF16),
-                pltpu.VMEM((nc, piece, wide), F32),
-                pltpu.VMEM((nc, piece, wide), F32),
-                pltpu.VMEM((piece, wide), F32),
-                pltpu.VMEM((nb, nc, nz, piece, wide), F32),
+                pltpu.VMEM((rows // 2, wide), F32),
+                pltpu.VMEM((nc, rows // 2, wide), F32),
+                pltpu.VMEM((rows // 2, wide), F32),
+                pltpu.VMEM((nb, nz, rows // 2, wide), F32),
                 pltpu.VMEM((CHUNKS, nz, slots, m // CHUNKS), BF16),
                 pltpu.VMEM((CHUNKS, nz, slots, m // CHUNKS), BF16),
                 dma((2,)), dma((3,)), dma((nb - 1,)),
@@ -425,7 +410,7 @@
                 dma((nc - 1,)), dma((nc,)),
                 dma((nb - 1, nz)), dma((nb, nz)),
                 dma((nc - 1,)), dma((nc,)),
-                dma((nb, nc, nz)), dma((nb, nc, nz)),
+                dma((nb, nz)), dma((nb, nz)),
                 dma((CHUNKS, nz - 1)), dma((CHUNKS, nz)),
                 dma((CHUNKS,)), dma((CHUNKS,)),
                 dma((nz // 2 - 1, CHUNKS)), dma((nz // 2 - 1, CHUNKS)),

time: 33.6 us -> 32.2 us (0.958)
  Pallas kernels: 31.9 us -> 30.5 us
    pallas_call x1, Pallas kernels: 31.9 us -> 30.5 us  [body(): pl.pallas_call(functools.partial(kernel, nb, nc, nz, width), out_shape=ja...]
where the time goes in v4:
time: 32.2 us; the launch traced here: 32.1 us
  Pallas kernels  30.5 us (95%)
  local copies, waits for them, and re-layouts  1.57 us (5%)
    pallas_call x1, Pallas kernels, body(): pl.pallas_call(functools.partial(kernel, nb, nc, nz, width), out_shape=ja...  30.5 us
    unnamed x1, local copies, waits for them, and re-layouts  1.57 us

profile of v4, /device:TPU:2, one launch (start us, length us, event | category | flops | bytes accessed | tf_op | source)
XLA Modules:
  0.0 32.1 jit_solution(1061605109091035180)
XLA Ops:
  0.0 30.5 %shard_map.64 = f32[1,16,2048]{2,1,0:T(8,128)} custom-call(f32[1,16,2048]{2,1,0:T(8,128)} %rhs_ref.1, f32[1,16,2048]{2,1,0:T(8,128)} %guess_ref.1, bf16[1,2048,2048]{2,1,0:T(8,128)(2,1)} %inv_ref.1, bf16[1,2,64,2048]{3,2,1,0:T(8,128)(2,1)} %left_ref.1, bf16[1,2,64,2048]{3,2,1,0:T(8,128)(2,1)} %right_ref.1, s32[2,2]{1,0:T(2,128)} %ranks_ref.1), custom_call_target="tpu_custom_call" | custom-call | tf_op jit(solution)/shard_map/pallas_call | solution.py:374
  30.5 1.6 %copy.8 = f32[1,16,2048]{2,1,0:T(8,128)} copy(f32[1,16,2048]{2,1,0:T(8,128)} %shard_map.64) | data formatting | bytes 262144
